TPU v7x, 256 devices: a whole 4x4x8 slice. The times are simulated.
256 devices in a mesh: section: 8 (over y, core), dp: 32 (over z, x).
Axes of the slice: x: 4, y: 4, z: 8, core: 2. Of those that a mesh axis runs over, the one named last changes fastest.
Arguments:
- hidden_in: bfloat16 [4, 1024, 8192], P(None, 'dp'), may hold values from -6 to 6
- cotangent: bfloat16 [4, 1024, 8192], P(None, 'dp'), may hold values from -6 to 6
- adapter_in: bfloat16 [8, 8192, 128], P('section', 'dp'), may hold values from -0.0625 to 0.0625
- adapter_out: bfloat16 [8, 128, 8192], P('section', None, 'dp'), may hold values from -0.5 to 0.5
- norm_gain: bfloat16 [8, 8192], P('section', 'dp'), may hold values from 0.5 to 1.5
- user_of_row: int32 [4, 1024], P(None, 'dp'), may hold values from 0 to 63, as said below
- included: int32 [4, 64], P(None, 'dp'), may hold values 0 or 1
Outputs:
- grad_in: float32 [8, 8192, 128], P('section', 'dp')
- grad_out: float32 [8, 128, 8192], P('section', None, 'dp')
- user_weights: float32 [4, 64], P(None, 'dp')
Inputs may be any that keep to these rules, and one draw needn't show every extreme that they name: `user_of_row`: within one micro-batch, the rows of the j-th block of 32 rows belong to users j * 2 to j * 2 + 1, in rising order, each of them with one row or more.
All inputs are finite; a program needn't handle non-finite values. No bound on the sum of `included` on one device may be relied on, other than what follows from the above.
Results may differ from a plain program's by a relative error of at most 0.018.
Values may be sent and summed in bfloat16 or wider, within the bound.
A program may use at most 64 MiB of HBM per device.

v0:
```python
import math
import jax
import jax.numpy as jnp
from jax import lax
from jax.sharding import Mesh
from jax.sharding import PartitionSpec as P

F32 = jnp.float32
BF = jnp.bfloat16


def mm(a, b, ca, cb):
    return lax.dot_general(a, b, (((ca,), (cb,)), ((), ())), preferred_element_type=F32)


def swap_route(n, m):
    return [(i * m + j, j * m + i) for i in range(n) for j in range(m)]


def recurrence(z0, y0, c0, norm0, gram, width):
    layers, rows, rank = z0.shape
    z = [z0[l] for l in range(layers)]
    y = [y0[l] for l in range(layers)]
    c = [c0[l] for l in range(layers)]
    square = norm0
    lows, rinvs, fulls, seen = ([], [], [], [])
    for l in range(layers):
        rinv = lax.rsqrt(square / width + 1e-05)
        full = z[l] * rinv
        low = full.astype(BF)
        seen.append(list(y))
        for j in range(layers):
            both = mm(low, gram[l, j], 1, 0)
            z[j] = z[j] + both[:, :rank]
            y[j] = y[j] + both[:, rank:]
        square = square + jnp.sum(low.astype(F32) * (seen[l][l] + y[l]), -1, keepdims=True)
        lows.append(low)
        rinvs.append(rinv)
        fulls.append(full)
    errs, cors = ([None] * layers, [None] * layers)
    for l in range(layers - 1, -1, -1):
        err = c[l].astype(BF)
        mean = jnp.sum(err.astype(F32) * fulls[l], -1, keepdims=True) / width
        cor = rinvs[l] * rinvs[l] * mean
        for j in range(l):
            c[j] = c[j] + rinvs[l] * mm(err, gram[j, l][:, :rank], 1, 1) - cor * seen[l][j]
        errs[l] = err
        cors[l] = cor
    return (lows, errs, rinvs, cors)


def shards(hidden_in, cotangent, adapter_in, adapter_out, norm_gain, user_of_row, included):
    n_s, n_z, n_x = (lax.axis_size(a) for a in ("section", "z", "x"))
    s, zi, xi = (lax.axis_index(a) for a in ("section", "z", "x"))
    plane = ("section", "x")
    layers = n_s
    micro, rows, width = hidden_in.shape
    cols, rank = adapter_in.shape[1:]
    users = included.shape[1]
    dev_rows = micro * rows
    group_rows = dev_rows * n_x
    own_rows = group_rows // (n_s * n_x)
    gain = norm_gain[0]
    a = adapter_in[0]
    bt = adapter_out[0].T
    g = (a.astype(F32) * gain.astype(F32)[:, None]).astype(BF)
    w = jnp.concatenate([jnp.concatenate([g, bt], 1), jnp.broadcast_to(gain[None], (16, cols))], 0)
    w = lax.ppermute(w, ("section", "z"), swap_route(n_s, n_z))
    w = lax.all_gather(w, "z")
    gains = w[:, cols].astype(F32)
    w = w[:, :cols]
    base = (zi * n_x + xi) * users
    key = (user_of_row - base + users * jnp.arange(micro, dtype=jnp.int32)[:, None]).reshape(
        dev_rows
    )
    onehot = (user_of_row - base)[:, :, None] == jnp.arange(users, dtype=jnp.int32)
    inc = jnp.sum(jnp.where(onehot, included[:, None, :], 0), -1).reshape(dev_rows)
    info = jnp.stack([key, inc]).astype(BF)
    info_all = lax.all_gather(info, "x")
    span = n_x * cols
    both = jnp.concatenate(
        [hidden_in.reshape(dev_rows, width), cotangent.reshape(dev_rows, width)], 0
    )
    both = lax.dynamic_slice_in_dim(both, s * span, span, 1)
    both = jnp.moveaxis(both.reshape(2 * dev_rows, n_x, cols), 1, 0)
    both = lax.all_to_all(both, "x", 0, 0, tiled=True)
    x = both[:, :dev_rows].reshape(group_rows, cols)
    cot = both[:, dev_rows:].reshape(group_rows, cols)
    own = lax.dynamic_index_in_dim(w, zi, 0, keepdims=False)[:, rank:]
    zy = jnp.stack([mm(x, w[l], 1, 0) for l in range(layers)])
    ct = jnp.stack([mm(cot, w[l][:, rank:], 1, 0) for l in range(layers)])
    proj = jnp.concatenate([zy, ct], -1).astype(BF)
    gram = jnp.stack([mm(own, w[l], 0, 0) for l in range(layers)]).astype(BF)
    n_plane = n_s * n_x
    proj = jnp.moveaxis(proj.reshape(layers, n_plane, own_rows, 3 * rank), 1, 0)
    gram = gram.reshape(n_plane, rank // n_x, 2 * rank)
    xf = x.astype(F32)
    norm0 = jnp.sum(xf * xf, -1).reshape(n_plane, own_rows, 1)
    proj = jnp.sum(lax.all_to_all(proj, plane, 0, 0, tiled=True).astype(F32), 0)
    gram = jnp.sum(lax.all_to_all(gram, plane, 0, 0, tiled=True).astype(F32), 0).astype(BF)
    norm0 = jnp.sum(lax.all_to_all(norm0, plane, 0, 0, tiled=True), 0)
    gram = lax.all_gather(gram, ("z", "section", "x"))
    gram = gram.reshape(layers, layers, rank, 2 * rank)
    lows, errs, rinvs, cors = recurrence(
        proj[..., :rank], proj[..., rank : 2 * rank], proj[..., 2 * rank :], norm0, gram, width
    )
    pack = jnp.stack(lows + errs)
    scal = jnp.concatenate(rinvs + cors, 1)
    pack = lax.all_gather(pack, plane, axis=1, tiled=True)
    scal = lax.all_gather(scal, plane, axis=0, tiled=True)
    low, err = (pack[:layers], pack[layers:])
    h = x.astype(F32)
    normed = []
    hs = []
    for l in range(layers):
        hs.append(h.astype(BF))
        normed.append((h * scal[:, l : l + 1] * gains[l][None]).astype(BF))
        h = h + mm(low[l], w[l][:, rank:], 1, 1)
    delta = cot.astype(F32)
    deltas = [None] * layers
    for l in range(layers - 1, -1, -1):
        deltas[l] = delta.astype(BF)
        delta = (
            delta
            + scal[:, l : l + 1] * mm(err[l], w[l][:, :rank], 1, 1)
            - scal[:, layers + l : layers + l + 1] * hs[l].astype(F32)
        )
    totals = []
    for i in range(n_x):
        at = slice(i * dev_rows, (i + 1) * dev_rows)
        keys = info_all[i, 0]
        same = keys[:, None] == keys[None, :]
        pairs = 0.0
        for l in range(layers):
            n, e, lo, d = (normed[l][at], err[l][at], low[l][at], deltas[l][at])
            pairs = pairs + mm(n, n, 1, 1) * mm(e, e, 1, 1) + mm(lo, lo, 1, 1) * mm(d, d, 1, 1)
        rowsum = jnp.sum(jnp.where(same, pairs, 0.0), -1)
        totals.append(jnp.sum(jnp.where(same, rowsum[None, :], 0.0), -1))
    totals = lax.psum(jnp.stack(totals), plane)
    bound = 0.8 * math.sqrt(layers * (rows // users) * width * width)
    row_w = info_all[:, 1].astype(F32) * (bound / jnp.maximum(jnp.sqrt(totals), bound))
    mine = lax.dynamic_index_in_dim(row_w, xi, 0, keepdims=False).reshape(micro, rows)
    user_weights = jnp.max(jnp.where(onehot, mine[:, :, None], 0.0), 1)
    row_w = row_w.reshape(group_rows, 1)
    grads = []
    for l in range(layers):
        we = (row_w * err[l].astype(F32)).astype(BF)
        wl = (row_w * low[l].astype(F32)).astype(BF)
        grads.append(jnp.concatenate([mm(normed[l], we, 0, 0), mm(deltas[l], wl, 0, 0)], 1))
    grads = jnp.stack(grads).astype(BF)
    grads = jnp.sum(lax.all_to_all(grads, "z", 0, 0, tiled=True).astype(F32), 0)
    grads = lax.ppermute(grads, ("section", "z"), swap_route(n_s, n_z))
    return (grads[None, :, :rank], grads[:, rank:].T[None], user_weights)


def solution(mesh):
    torus = Mesh(mesh.devices.reshape(mesh.shape["section"], 8, 4), ("section", "z", "x"))
    dp = ("z", "x")
    return jax.shard_map(
        shards,
        mesh=torus,
        in_specs=(
            P(None, dp, None),
            P(None, dp, None),
            P("section", dp, None),
            P("section", None, dp),
            P("section", dp),
            P(None, dp),
            P(None, dp),
        ),
        out_specs=(P("section", dp, None), P("section", None, dp), P(None, dp)),
        check_vma=False,
    )
```

profile of v0, /device:TPU:25, one launch (start us, length us, event | category | flops | bytes accessed | tf_op | source)
XLA Modules:
  0.0 460.0 jit_solution(16412173527792185459)
XLA Ops:
  9.9 7.7 %collective-permute-start = (bf16[272,256]{1,0:T(8,128)(2,1)S(1)}, bf16[272,256]{1,0:T(8,128)(2,1)S(1)}, u32[]{:S(2)}, u32[]{:S(2)}) collective-permute-start(bf16[272,256]{1,0:T(8,128)(2,1)S(1)} %pad_maximum_fusion), channel_id=1, source_target_pairs={{0,0},{4,32},{8,64},{12,96},{16,128},{20,160},{24,192},{28,224},{3... | collective-permute-start | bytes 417800 | tf_op jit(solution)/shard_map/ppermute | solution.py:68
  17.6 10.1 %collective-permute-done = bf16[272,256]{1,0:T(8,128)(2,1)S(1)} collective-permute-done((bf16[272,256]{1,0:T(8,128)(2,1)S(1)}, bf16[272,256]{1,0:T(8,128)(2,1)S(1)}, u32[]{:S(2)}, u32[]{:S(2)}) %collective-permute-start) | collective-permute-done | bytes 139296 | tf_op jit(solution)/shard_map/ppermute | solution.py:68
  28.4 33.7 %all-gather.8.cloned.1.call-done = bf16[2176,256]{1,0:T(8,128)(2,1)} async-done(((bf16[272,256]{1,0:T(8,128)(2,1)}), bf16[2176,256]{1,0:T(8,128)(2,1)}) %all-gather.8.cloned.1.call-update) | async-done | bytes 1114128 | tf_op jit(solution)/shard_map/all_gather | solution.py:69
  66.1 12.5 %all-to-all-start.3 = ((bf16[32,32,256]{2,1,0:T(8,128)(2,1)}), bf16[32,32,256]{2,1,0:T(8,128)(2,1)}, u32[]{:S(2)}, u32[]{:S(2)}) async-start(bf16[32,32,256]{2,1,0:T(8,128)(2,1)} %bitcast.1095), calls=%async_computation.3 | async-start | bytes 1048576 | tf_op jit(solution)/shard_map/all_to_all | solution.py:100
  78.6 1.8 fusion.201
  80.4 2.0 copy.59
  82.4 5.8 %all-to-all-done.3 = bf16[32,32,256]{2,1,0:T(8,128)(2,1)} async-done(((bf16[32,32,256]{2,1,0:T(8,128)(2,1)}), bf16[32,32,256]{2,1,0:T(8,128)(2,1)}, u32[]{:S(2)}, u32[]{:S(2)}) %all-to-all-start.3) | async-done | bytes 524320 | tf_op jit(solution)/shard_map/all_to_all | solution.py:100
  88.3 3.5 all-to-all-start
  91.8 1.7 reduce_sum.273
  93.6 7.3 %all-to-all-done = bf16[4,256,256]{1,2,0:T(8,128)(2,1)S(1)} async-done(((bf16[4,256,256]{1,2,0:T(8,128)(2,1)}), bf16[4,256,256]{1,2,0:T(8,128)(2,1)S(1)}, u32[]{:S(2)}, u32[]{:S(2)}) %all-to-all-start) | async-done | bytes 524320 | tf_op jit(solution)/shard_map/all_to_all | solution.py:86
  101.7 6.6 %all-to-all-start.1 = ((f32[32,16,1]{1,2,0:T(1,128)}), f32[32,16,1]{1,2,0:T(1,128)S(1)}, u32[]{:S(2)}, u32[]{:S(2)}) async-start(f32[32,16,1]{1,2,0:T(1,128)} %bitcast.4), calls=%async_computation.1 | async-start | bytes 32768 | tf_op jit(solution)/shard_map/all_to_all | solution.py:101
  113.2 2.2 copy.64
  115.4 7.4 %all-to-all-start.2 = ((bf16[32,8,16,384]{3,2,1,0:T(8,128)(2,1)}), bf16[32,8,16,384]{3,2,1,0:T(8,128)(2,1)}, u32[]{:S(2)}, u32[]{:S(2)}) async-start(bf16[32,8,16,384]{3,2,1,0:T(8,128)(2,1)} %copy.64), calls=%async_computation.2 | async-start | bytes 6291456 | tf_op jit(solution)/shard_map/all_to_all | solution.py:99
  123.0 38.1 %all-to-all-done.2 = bf16[32,8,16,384]{3,2,1,0:T(8,128)(2,1)} async-done(((bf16[32,8,16,384]{3,2,1,0:T(8,128)(2,1)}), bf16[32,8,16,384]{3,2,1,0:T(8,128)(2,1)}, u32[]{:S(2)}, u32[]{:S(2)}) %all-to-all-start.2) | async-done | bytes 3145760 | tf_op jit(solution)/shard_map/all_to_all | solution.py:99
  161.1 2.3 convert_reduce_fusion
  163.5 50.2 %all-gather.10.cloned.1.call-done = bf16[8192,256]{1,0:T(8,128)(2,1)} async-done(((bf16[32,256]{1,0:T(8,128)(2,1)}), bf16[8192,256]{1,0:T(8,128)(2,1)}) %all-gather.10.cloned.1.call-update) | async-done | bytes 4194320 | tf_op jit(solution)/shard_map/all_gather | solution.py:102
  213.7 1.5 slice_bitcast_fusion.99
  243.6 6.6 %all_gather.27 = bf16[4,2,128]{2,1,0:T(2,128)(2,1)S(1)} all-gather(bf16[1,2,128]{2,1,0:T(2,128)(2,1)S(1)} %pad_maximum_fusion.2), channel_id=1, replica_groups=mesh['section'=8,'z'=8,'x'=4] {'x'}, dimensions={0}, use_global_device_ids=true | all-gather | bytes 2560 | tf_op jit(solution)/shard_map/all_gather | solution.py:79
  251.9 45.5 %all_gather.26 = f32[512,16]{1,0:T(8,128)S(1)} all-gather(f32[16,16]{1,0:T(8,128)S(1)} %copy.65), channel_id=1, replica_groups=mesh['section'=8,'z'=8,'x'=4] {'section','x'}, dimensions={0}, use_global_device_ids=true | all-gather | bytes 33792 | tf_op jit(solution)/shard_map/all_gather | solution.py:110
  297.4 2.6 slice_reduce_fusion.14
  332.2 55.6 %psum.7 = f32[4,128]{1,0:T(4,128)S(1)} all-reduce(f32[4,128]{1,0:T(4,128)S(1)} %pad_maximum_fusion.1), channel_id=1, replica_groups=mesh['section'=8,'z'=8,'x'=4] {'section','x'}, use_global_device_ids=true, to_apply=%region_28.29 | all-reduce | flops 512 | bytes 4096 | tf_op jit(solution)/shard_map/psum | solution.py:139
  397.4 30.1 %all_to_all.25 = bf16[8,256,256]{1,2,0:T(8,128)(2,1)S(1)} all-to-all(bf16[8,256,256]{1,2,0:T(8,128)(2,1)S(1)} %fusion.217), channel_id=1, replica_groups=mesh['section'=8,'z'=8,'x'=4] {'z'}, dimensions={0} | all-to-all | bytes 2097152 | tf_op jit(solution)/shard_map/all_to_all | solution.py:151
  427.7 8.4 %collective-permute-start.1 = (f32[256,256]{0,1:T(8,128)S(1)}, f32[256,256]{0,1:T(8,128)S(1)}, u32[]{:S(2)}, u32[]{:S(2)}) collective-permute-start(f32[256,256]{0,1:T(8,128)S(1)} %convert_reduce_fusion.1), channel_id=1, source_target_pairs={{0,0},{4,32},{8,64},{12,96},{16,128},{20,160},{24,192},{28,224},{3... | collective-permute-start | bytes 786440 | tf_op jit(solution)/shard_map/ppermute | solution.py:152
  436.9 15.1 %collective-permute-done.1 = f32[256,256]{0,1:T(8,128)S(1)} collective-permute-done((f32[256,256]{0,1:T(8,128)S(1)}, f32[256,256]{0,1:T(8,128)S(1)}, u32[]{:S(2)}, u32[]{:S(2)}) %collective-permute-start.1) | collective-permute-done | bytes 262176 | tf_op jit(solution)/shard_map/ppermute | solution.py:152
  (521 shorter events, 85.5 us)
Async XLA Ops:
  7.2 55.0 %all-gather.8.cloned.1.call-start = ((), (), s32[]{:S(2)}) async-start(), calls=%async_computation.6 | async-start | bytes 1253376 | tf_op jit(solution)/shard_map/all_gather | solution.py:69
  9.9 17.9 %collective-permute-start = (bf16[272,256]{1,0:T(8,128)(2,1)S(1)}, bf16[272,256]{1,0:T(8,128)(2,1)S(1)}, u32[]{:S(2)}, u32[]{:S(2)}) collective-permute-start(bf16[272,256]{1,0:T(8,128)(2,1)S(1)} %pad_maximum_fusion), channel_id=1, source_target_pairs={{0,0},{4,32},{8,64},{12,96},{16,128},{20,160},{24,192},{28,224},{3... | collective-permute-start | bytes 417800 | tf_op jit(solution)/shard_map/ppermute | solution.py:68
  63.5 15.0 %copy-start.6 = (bf16[4,32,8192]{2,1,0:T(8,128)(2,1)S(1)}, bf16[4,32,8192]{2,1,0:T(8,128)(2,1)}, u32[]{:S(2)}) copy-start(bf16[4,32,8192]{2,1,0:T(8,128)(2,1)} %param.7) | copy-start | bytes 6291460
  66.1 22.2 %all-to-all-start.3 = ((bf16[32,32,256]{2,1,0:T(8,128)(2,1)}), bf16[32,32,256]{2,1,0:T(8,128)(2,1)}, u32[]{:S(2)}, u32[]{:S(2)}) async-start(bf16[32,32,256]{2,1,0:T(8,128)(2,1)} %bitcast.1095), calls=%async_computation.3 | async-start | bytes 1048576 | tf_op jit(solution)/shard_map/all_to_all | solution.py:100
  88.3 12.6 %all-to-all-start = ((bf16[4,256,256]{1,2,0:T(8,128)(2,1)}), bf16[4,256,256]{1,2,0:T(8,128)(2,1)S(1)}, u32[]{:S(2)}, u32[]{:S(2)}) async-start(bf16[4,256,256]{1,2,0:T(8,128)(2,1)} %bitcast.3), calls=%async_computation | async-start | bytes 1048576 | tf_op jit(solution)/shard_map/all_to_all | solution.py:86
  91.8 122.0 %all-gather.10.cloned.1.call-start = ((), (), s32[]{:S(2)}) async-start(), calls=%async_computation.7 | async-start | bytes 4210688 | tf_op jit(solution)/shard_map/all_gather | solution.py:102
  100.9 199.1 %copy-start.3 = (bf16[4,256,256]{1,2,0:T(8,128)(2,1)}, bf16[4,256,256]{1,2,0:T(8,128)(2,1)S(1)}, u32[]{:S(2)}) copy-start(bf16[4,256,256]{1,2,0:T(8,128)(2,1)S(1)} %all-to-all-done) | copy-start | bytes 1572868
  101.7 13.7 %all-to-all-start.1 = ((f32[32,16,1]{1,2,0:T(1,128)}), f32[32,16,1]{1,2,0:T(1,128)S(1)}, u32[]{:S(2)}, u32[]{:S(2)}) async-start(f32[32,16,1]{1,2,0:T(1,128)} %bitcast.4), calls=%async_computation.1 | async-start | bytes 32768 | tf_op jit(solution)/shard_map/all_to_all | solution.py:101
  115.4 45.6 %all-to-all-start.2 = ((bf16[32,8,16,384]{3,2,1,0:T(8,128)(2,1)}), bf16[32,8,16,384]{3,2,1,0:T(8,128)(2,1)}, u32[]{:S(2)}, u32[]{:S(2)}) async-start(bf16[32,8,16,384]{3,2,1,0:T(8,128)(2,1)} %copy.64), calls=%async_computation.2 | async-start | bytes 6291456 | tf_op jit(solution)/shard_map/all_to_all | solution.py:99
  122.8 180.8 %all-gather.6.cloned.1.call-start = ((), (), s32[]{:S(2)}) async-start(), calls=%async_computation.5 | async-start | bytes 2162688 | tf_op jit(solution)/shard_map/all_gather | solution.py:109
  213.7 17.7 %copy-start.2 = (bf16[8192,256]{1,0:T(8,128)(2,1)S(1)}, bf16[8192,256]{1,0:T(8,128)(2,1)}, u32[]{:S(2)}) copy-start(bf16[8192,256]{1,0:T(8,128)(2,1)} %all-gather.10.cloned.1.call-done) | copy-start | bytes 12582916
  251.5 52.1 %copy-start.5 = (f32[4,128,256]{2,1,0:T(8,128)}, f32[4,128,256]{2,1,0:T(8,128)S(1)}, u32[]{:S(2)}) copy-start(f32[4,128,256]{2,1,0:T(8,128)S(1)} %copy.68) | copy-start | bytes 1572868
  300.0 9.1 %copy-start.56 = (f32[512]{0:T(512)}, f32[512]{0:T(512)S(1)}, u32[]{:S(2)}) copy-start(f32[512]{0:T(512)S(1)} %get-tuple-element.19) | copy-start | bytes 6148
  300.0 9.7 %copy-start.58 = (f32[512]{0:T(512)}, f32[512]{0:T(512)S(1)}, u32[]{:S(2)}) copy-start(f32[512]{0:T(512)S(1)} %get-tuple-element.21) | copy-start | bytes 6148
  314.0 17.4 %copy-start.20 = (bf16[512,256]{1,0:T(8,128)(2,1)}, bf16[512,256]{1,0:T(8,128)(2,1)S(1)}, u32[]{:S(2)}) copy-start(bf16[512,256]{1,0:T(8,128)(2,1)S(1)} %get-tuple-element.197) | copy-start | bytes 786436
  314.3 16.6 %copy-start.22 = (bf16[512,256]{1,0:T(8,128)(2,1)}, bf16[512,256]{1,0:T(8,128)(2,1)S(1)}, u32[]{:S(2)}) copy-start(bf16[512,256]{1,0:T(8,128)(2,1)S(1)} %get-tuple-element.193) | copy-start | bytes 786436
  314.6 15.8 %copy-start.24 = (bf16[512,256]{1,0:T(8,128)(2,1)}, bf16[512,256]{1,0:T(8,128)(2,1)S(1)}, u32[]{:S(2)}) copy-start(bf16[512,256]{1,0:T(8,128)(2,1)S(1)} %get-tuple-element.189) | copy-start | bytes 786436
  315.0 14.9 %copy-start.26 = (bf16[512,256]{1,0:T(8,128)(2,1)}, bf16[512,256]{1,0:T(8,128)(2,1)S(1)}, u32[]{:S(2)}) copy-start(bf16[512,256]{1,0:T(8,128)(2,1)S(1)} %get-tuple-element.185) | copy-start | bytes 786436
  315.3 14.1 %copy-start.28 = (bf16[512,256]{1,0:T(8,128)(2,1)}, bf16[512,256]{1,0:T(8,128)(2,1)S(1)}, u32[]{:S(2)}) copy-start(bf16[512,256]{1,0:T(8,128)(2,1)S(1)} %get-tuple-element.181) | copy-start | bytes 786436
  315.9 13.0 %copy-start.29 = (bf16[512,256]{1,0:T(8,128)(2,1)}, bf16[512,256]{1,0:T(8,128)(2,1)S(1)}, u32[]{:S(2)}) copy-start(bf16[512,256]{1,0:T(8,128)(2,1)S(1)} %get-tuple-element.177) | copy-start | bytes 786436
  328.6 59.2 %copy-start.62 = (bf16[4,1,128]{2,1,0:T(2,128)(2,1)S(1)}, bf16[4,1,128]{2,1,0:T(2,128)(2,1)}, u32[]{:S(2)}) copy-start(bf16[4,1,128]{2,1,0:T(2,128)(2,1)} %slice.2329) | copy-start | bytes 3076
  330.2 60.6 %copy-start.14 = (bf16[512,256]{1,0:T(8,128)(2,1)S(1)}, bf16[512,256]{1,0:T(8,128)(2,1)}, u32[]{:S(2)}) copy-start(bf16[512,256]{1,0:T(8,128)(2,1)} %copy-done.13) | copy-start | bytes 786436
  332.1 61.8 %copy-start.27 = (bf16[512,256]{1,0:T(8,128)(2,1)S(1)}, bf16[512,256]{1,0:T(8,128)(2,1)}, u32[]{:S(2)}) copy-start(bf16[512,256]{1,0:T(8,128)(2,1)} %copy-done.26) | copy-start | bytes 786436
  427.7 24.3 %collective-permute-start.1 = (f32[256,256]{0,1:T(8,128)S(1)}, f32[256,256]{0,1:T(8,128)S(1)}, u32[]{:S(2)}, u32[]{:S(2)}) collective-permute-start(f32[256,256]{0,1:T(8,128)S(1)} %convert_reduce_fusion.1), channel_id=1, source_target_pairs={{0,0},{4,32},{8,64},{12,96},{16,128},{20,160},{24,192},{28,224},{3... | collective-permute-start | bytes 786440 | tf_op jit(solution)/shard_map/ppermute | solution.py:152
  (59 other events, 180.6 us)
Sparse Core Ops, SparseCore 0:
  28.5 33.5 all-gather.7
  96.3 117.3 all-gather.9
  243.3 46.5 all-gather.5
where the time goes:
time: 462 us; the launch traced here: 460 us
  waiting for transfers between devices  161 us (35%)
  blocking collectives  138 us (30%)
  matrix products  68.7 us (15%)
  starting transfers between devices  46.2 us (10%)
  local copies, waits for them, and re-layouts  19.8 us (4%)
  between operations  15.9 us (3%)
  other arithmetic  11.1 us (2%)
    dot_general x266, matrix products, mm(): lax.dot_general(a, b, (((ca,), (cb,)), ((), ())), preferred_element_type=...  68.7 us
    psum x1, blocking collectives, shards(): totals = lax.psum(jnp.stack(totals), plane)  55.6 us
    all_gather x1, waiting for transfers between devices, shards(): gram = lax.all_gather(gram, ('z', 'section', 'x'))  50.2 us
    all_gather x1, blocking collectives, shards(): scal = lax.all_gather(scal, plane, axis=0, tiled=True)  45.5 us
    all_to_all x1, waiting for transfers between devices, shards(): proj = jnp.sum(lax.all_to_all(proj, plane, 0, 0, tiled=True).astype(F32), 0)  38.1 us
    all_gather x1, waiting for transfers between devices, shards(): w = lax.all_gather(w, 'z')  33.7 us
    all_to_all x1, blocking collectives, shards(): grads = jnp.sum(lax.all_to_all(grads, 'z', 0, 0, tiled=True).astype(F32), 0)  30.1 us
    ppermute x1, waiting for transfers between devices, shards(): grads = lax.ppermute(grads, ('section', 'z'), swap_route(n_s, n_z))  15.1 us
  transfers between devices with their start and end apart: 9, of which 7 were waited for; matrix products, arithmetic and copies ran while one was open for 5% of the time, Pallas kernels for 0%

commit v1 on v0

--- a/solution.py
+++ b/solution.py
@@ -136,7 +136,7 @@
             pairs = pairs + mm(n, n, 1, 1) * mm(e, e, 1, 1) + mm(lo, lo, 1, 1) * mm(d, d, 1, 1)
         rowsum = jnp.sum(jnp.where(same, pairs, 0.0), -1)
         totals.append(jnp.sum(jnp.where(same, rowsum[None, :], 0.0), -1))
-    totals = lax.psum(jnp.stack(totals), plane)
+    totals = jnp.sum(lax.all_gather(jnp.stack(totals), plane), axis=0)
     bound = 0.8 * math.sqrt(layers * (rows // users) * width * width)
     row_w = info_all[:, 1].astype(F32) * (bound / jnp.maximum(jnp.sqrt(totals), bound))
     mine = lax.dynamic_index_in_dim(row_w, xi, 0, keepdims=False).reshape(micro, rows)

time: 462 us -> 470 us (1.017)
  blocking collectives: 138 us -> 93.3 us
  waiting for transfers between devices: 161 us -> 195 us
  other arithmetic: 11.1 us -> 23.6 us
    psum x1 -> x0, blocking collectives: 55.6 us -> none  [shards(): totals = lax.psum(jnp.stack(totals), plane)]
    all_gather x0 -> x1, blocking collectives: none -> 41.3 us  [shards(): totals = jnp.sum(lax.all_gather(jnp.stack(totals), plane), axis=0)]
    all_to_all x1 -> x0, blocking collectives: 30.1 us -> none  [shards(): grads = jnp.sum(lax.all_to_all(grads, 'z', 0, 0, tiled=True).astype(F32), 0)]
    all_to_all x0 -> x1, waiting for transfers between devices: none -> 29.3 us  [shards(): grads = jnp.sum(lax.all_to_all(grads, 'z', 0, 0, tiled=True).astype(F32), 0)]
    unnamed x15 -> x16, other arithmetic: 1.35 us -> 10 us
    ppermute x1, waiting for transfers between devices: 15.1 us -> 21.6 us  [shards(): grads = lax.ppermute(grads, ('section', 'z'), swap_route(n_s, n_z))]
    ppermute x1, starting transfers between devices: 8.41 us -> 1.92 us  [shards(): grads = lax.ppermute(grads, ('section', 'z'), swap_route(n_s, n_z))]
  transfers between devices with their start and end apart: 9 -> 10, of which waited for: 7 -> 8; matrix products, arithmetic and copies ran while one was open for 5% -> 6% of each run, Pallas kernels for 0% -> 0%
where the time goes in v1:
time: 470 us; the launch traced here: 468 us
  waiting for transfers between devices  195 us (41%)
  blocking collectives  93.3 us (20%)
  matrix products  73.2 us (16%)
  starting transfers between devices  43.6 us (9%)
  other arithmetic  23.6 us (5%)
  local copies, waits for them, and re-layouts  23.2 us (5%)
  between operations  15.8 us (3%)
    dot_general x266, matrix products, mm(): lax.dot_general(a, b, (((ca,), (cb,)), ((), ())), preferred_element_type=...  73.2 us
    all_gather x1, waiting for transfers between devices, shards(): gram = lax.all_gather(gram, ('z', 'section', 'x'))  49.6 us
    all_gather x1, blocking collectives, shards(): scal = lax.all_gather(scal, plane, axis=0, tiled=True)  45.4 us
    all_gather x1, blocking collectives, shards(): totals = jnp.sum(lax.all_gather(jnp.stack(totals), plane), axis=0)  41.3 us
    all_to_all x1, waiting for transfers between devices, shards(): proj = jnp.sum(lax.all_to_all(proj, plane, 0, 0, tiled=True).astype(F32), 0)  37.6 us
    all_gather x1, waiting for transfers between devices, shards(): w = lax.all_gather(w, 'z')  33.7 us
    all_to_all x1, waiting for transfers between devices, shards(): grads = jnp.sum(lax.all_to_all(grads, 'z', 0, 0, tiled=True).astype(F32), 0)  29.3 us
    ppermute x1, waiting for transfers between devices, shards(): grads = lax.ppermute(grads, ('section', 'z'), swap_route(n_s, n_z))  21.6 us
  transfers between devices with their start and end apart: 10, of which 8 were waited for; matrix products, arithmetic and copies ran while one was open for 6% of the time, Pallas kernels for 0%

profile of v1, /device:TPU:25, one launch (start us, length us, event | category | flops | bytes accessed | tf_op | source)
XLA Modules:
  0.0 468.0 jit_solution(15670037394526673433)
XLA Ops:
  9.9 7.7 %collective-permute-start = (bf16[272,256]{1,0:T(8,128)(2,1)S(1)}, bf16[272,256]{1,0:T(8,128)(2,1)S(1)}, u32[]{:S(2)}, u32[]{:S(2)}) collective-permute-start(bf16[272,256]{1,0:T(8,128)(2,1)S(1)} %pad_maximum_fusion), channel_id=1, source_target_pairs={{0,0},{4,32},{8,64},{12,96},{16,128},{20,160},{24,192},{28,224},{3... | collective-permute-start | bytes 417800 | tf_op jit(solution)/shard_map/ppermute | solution.py:68
  17.6 10.1 %collective-permute-done = bf16[272,256]{1,0:T(8,128)(2,1)S(1)} collective-permute-done((bf16[272,256]{1,0:T(8,128)(2,1)S(1)}, bf16[272,256]{1,0:T(8,128)(2,1)S(1)}, u32[]{:S(2)}, u32[]{:S(2)}) %collective-permute-start) | collective-permute-done | bytes 139296 | tf_op jit(solution)/shard_map/ppermute | solution.py:68
  28.4 33.7 %all-gather.10.cloned.1.call-done = bf16[2176,256]{1,0:T(8,128)(2,1)} async-done(((bf16[272,256]{1,0:T(8,128)(2,1)}), bf16[2176,256]{1,0:T(8,128)(2,1)}) %all-gather.10.cloned.1.call-update) | async-done | bytes 1114128 | tf_op jit(solution)/shard_map/all_gather | solution.py:69
  66.1 12.5 %all-to-all-start.3 = ((bf16[32,32,256]{2,1,0:T(8,128)(2,1)}), bf16[32,32,256]{2,1,0:T(8,128)(2,1)}, u32[]{:S(2)}, u32[]{:S(2)}) async-start(bf16[32,32,256]{2,1,0:T(8,128)(2,1)} %bitcast.1095), calls=%async_computation.3 | async-start | bytes 1048576 | tf_op jit(solution)/shard_map/all_to_all | solution.py:100
  78.6 1.8 fusion.201
  80.4 2.0 copy.57
  82.5 5.8 %all-to-all-done.3 = bf16[32,32,256]{2,1,0:T(8,128)(2,1)} async-done(((bf16[32,32,256]{2,1,0:T(8,128)(2,1)}), bf16[32,32,256]{2,1,0:T(8,128)(2,1)}, u32[]{:S(2)}, u32[]{:S(2)}) %all-to-all-start.3) | async-done | bytes 524320 | tf_op jit(solution)/shard_map/all_to_all | solution.py:100
  88.3 3.5 all-to-all-start
  91.8 1.7 reduce_sum.282
  93.6 7.3 %all-to-all-done = bf16[4,256,256]{1,2,0:T(8,128)(2,1)S(1)} async-done(((bf16[4,256,256]{1,2,0:T(8,128)(2,1)}), bf16[4,256,256]{1,2,0:T(8,128)(2,1)S(1)}, u32[]{:S(2)}, u32[]{:S(2)}) %all-to-all-start) | async-done | bytes 524320 | tf_op jit(solution)/shard_map/all_to_all | solution.py:86
  101.7 6.6 %all-to-all-start.1 = ((f32[32,16,1]{1,2,0:T(1,128)}), f32[32,16,1]{1,2,0:T(1,128)S(1)}, u32[]{:S(2)}, u32[]{:S(2)}) async-start(f32[32,16,1]{1,2,0:T(1,128)} %bitcast.4), calls=%async_computation.1 | async-start | bytes 32768 | tf_op jit(solution)/shard_map/all_to_all | solution.py:101
  113.1 2.2 copy.62
  115.4 7.4 %all-to-all-start.2 = ((bf16[32,8,16,384]{3,2,1,0:T(8,128)(2,1)}), bf16[32,8,16,384]{3,2,1,0:T(8,128)(2,1)}, u32[]{:S(2)}, u32[]{:S(2)}) async-start(bf16[32,8,16,384]{3,2,1,0:T(8,128)(2,1)} %copy.62), calls=%async_computation.2 | async-start | bytes 6291456 | tf_op jit(solution)/shard_map/all_to_all | solution.py:99
  123.5 37.6 %all-to-all-done.2 = bf16[32,8,16,384]{3,2,1,0:T(8,128)(2,1)} async-done(((bf16[32,8,16,384]{3,2,1,0:T(8,128)(2,1)}), bf16[32,8,16,384]{3,2,1,0:T(8,128)(2,1)}, u32[]{:S(2)}, u32[]{:S(2)}) %all-to-all-start.2) | async-done | bytes 3145760 | tf_op jit(solution)/shard_map/all_to_all | solution.py:99
  161.1 2.3 convert_reduce_fusion
  164.1 49.6 %all-gather.12.cloned.1.call-done = bf16[8192,256]{1,0:T(8,128)(2,1)} async-done(((bf16[32,256]{1,0:T(8,128)(2,1)}), bf16[8192,256]{1,0:T(8,128)(2,1)}) %all-gather.12.cloned.1.call-update) | async-done | bytes 4194320 | tf_op jit(solution)/shard_map/all_gather | solution.py:102
  254.4 6.6 %all_gather.33 = bf16[4,2,128]{2,1,0:T(2,128)(2,1)S(1)} all-gather(bf16[1,2,128]{2,1,0:T(2,128)(2,1)S(1)} %pad_maximum_fusion.1), channel_id=1, replica_groups=mesh['section'=8,'z'=8,'x'=4] {'x'}, dimensions={0}, use_global_device_ids=true | all-gather | bytes 2560 | tf_op jit(solution)/shard_map/all_gather | solution.py:79
  262.9 45.4 %all_gather.32 = f32[512,16]{1,0:T(8,128)S(1)} all-gather(f32[16,16]{1,0:T(8,128)S(1)} %copy.63), channel_id=1, replica_groups=mesh['section'=8,'z'=8,'x'=4] {'section','x'}, dimensions={0}, use_global_device_ids=true | all-gather | bytes 33792 | tf_op jit(solution)/shard_map/all_gather | solution.py:110
  308.4 2.6 slice_reduce_fusion.14
  343.5 41.3 %all-gather.3 = f32[32,4,128]{2,1,0:T(4,128)S(1)} all-gather(f32[1,4,128]{2,1,0:T(4,128)S(1)} %maximum_bitcast_fusion.9), channel_id=4, replica_groups=mesh['section'=8,'z'=8,'x'=4] {'section','x'}, dimensions={0}, use_global_device_ids=true | all-gather | bytes 67584 | tf_op jit(solution)/shard_map/all_gather | solution.py:139
  402.3 3.9 all-to-all-start.4
  406.2 29.3 %all-to-all-done.4 = bf16[8,256,256]{1,2,0:T(8,128)(2,1)S(1)} async-done(((bf16[8,256,256]{1,2,0:T(8,128)(2,1)}), bf16[8,256,256]{1,2,0:T(8,128)(2,1)S(1)}, u32[]{:S(2)}, u32[]{:S(2)}) %all-to-all-start.4) | async-done | bytes 1048608 | tf_op jit(solution)/shard_map/all_to_all | solution.py:151
  435.7 1.9 collective-permute-start.1
  438.4 21.6 %collective-permute-done.1 = f32[256,256]{0,1:T(8,128)S(1)} collective-permute-done((f32[256,256]{0,1:T(8,128)S(1)}, f32[256,256]{0,1:T(8,128)S(1)}, u32[]{:S(2)}, u32[]{:S(2)}) %collective-permute-start.1) | collective-permute-done | bytes 262176 | tf_op jit(solution)/shard_map/ppermute | solution.py:152
  (536 shorter events, 107.4 us)
Async XLA Ops:
  7.2 55.0 %all-gather.10.cloned.1.call-start = ((), (), s32[]{:S(2)}) async-start(), calls=%async_computation.6 | async-start | bytes 1253376 | tf_op jit(solution)/shard_map/all_gather | solution.py:69
  9.9 17.9 %collective-permute-start = (bf16[272,256]{1,0:T(8,128)(2,1)S(1)}, bf16[272,256]{1,0:T(8,128)(2,1)S(1)}, u32[]{:S(2)}, u32[]{:S(2)}) collective-permute-start(bf16[272,256]{1,0:T(8,128)(2,1)S(1)} %pad_maximum_fusion), channel_id=1, source_target_pairs={{0,0},{4,32},{8,64},{12,96},{16,128},{20,160},{24,192},{28,224},{3... | collective-permute-start | bytes 417800 | tf_op jit(solution)/shard_map/ppermute | solution.py:68
  66.1 22.2 %all-to-all-start.3 = ((bf16[32,32,256]{2,1,0:T(8,128)(2,1)}), bf16[32,32,256]{2,1,0:T(8,128)(2,1)}, u32[]{:S(2)}, u32[]{:S(2)}) async-start(bf16[32,32,256]{2,1,0:T(8,128)(2,1)} %bitcast.1095), calls=%async_computation.3 | async-start | bytes 1048576 | tf_op jit(solution)/shard_map/all_to_all | solution.py:100
  88.3 12.6 %all-to-all-start = ((bf16[4,256,256]{1,2,0:T(8,128)(2,1)}), bf16[4,256,256]{1,2,0:T(8,128)(2,1)S(1)}, u32[]{:S(2)}, u32[]{:S(2)}) async-start(bf16[4,256,256]{1,2,0:T(8,128)(2,1)} %bitcast.3), calls=%async_computation | async-start | bytes 1048576 | tf_op jit(solution)/shard_map/all_to_all | solution.py:86
  91.8 121.9 %all-gather.12.cloned.1.call-start = ((), (), s32[]{:S(2)}) async-start(), calls=%async_computation.7 | async-start | bytes 4210688 | tf_op jit(solution)/shard_map/all_gather | solution.py:102
  101.7 13.7 %all-to-all-start.1 = ((f32[32,16,1]{1,2,0:T(1,128)}), f32[32,16,1]{1,2,0:T(1,128)S(1)}, u32[]{:S(2)}, u32[]{:S(2)}) async-start(f32[32,16,1]{1,2,0:T(1,128)} %bitcast.4), calls=%async_computation.1 | async-start | bytes 32768 | tf_op jit(solution)/shard_map/all_to_all | solution.py:101
  115.4 45.7 %all-to-all-start.2 = ((bf16[32,8,16,384]{3,2,1,0:T(8,128)(2,1)}), bf16[32,8,16,384]{3,2,1,0:T(8,128)(2,1)}, u32[]{:S(2)}, u32[]{:S(2)}) async-start(bf16[32,8,16,384]{3,2,1,0:T(8,128)(2,1)} %copy.62), calls=%async_computation.2 | async-start | bytes 6291456 | tf_op jit(solution)/shard_map/all_to_all | solution.py:99
  122.8 192.4 %all-gather.8.cloned.1.call-start = ((), (), s32[]{:S(2)}) async-start(), calls=%async_computation.5 | async-start | bytes 2162688 | tf_op jit(solution)/shard_map/all_gather | solution.py:109
  123.4 94.1 %copy-start.66 = (f32[16]{0:T(128)}, f32[16]{0:T(128)S(1)}, u32[]{:S(2)}) copy-start(f32[16]{0:T(128)S(1)} %reduce_sum.280) | copy-start | bytes 196
  123.5 93.9 %copy-start.76 = (f32[16]{0:T(128)}, f32[16]{0:T(128)S(1)}, u32[]{:S(2)}) copy-start(f32[16]{0:T(128)S(1)} %add_rsqrt_fusion.7) | copy-start | bytes 196
  213.7 22.2 %copy-start.2 = (bf16[8192,256]{1,0:T(8,128)(2,1)S(1)}, bf16[8192,256]{1,0:T(8,128)(2,1)}, u32[]{:S(2)}) copy-start(bf16[8192,256]{1,0:T(8,128)(2,1)} %all-gather.12.cloned.1.call-done) | copy-start | bytes 12582916
  218.2 29.4 %copy-start.71 = (f32[16]{0:T(128)}, f32[16]{0:T(128)S(1)}, u32[]{:S(2)}) copy-start(f32[16]{0:T(128)S(1)} %get-tuple-element.37) | copy-start | bytes 196
  244.6 17.9 %copy-start.77 = (f32[16]{0:T(128)S(1)}, f32[16]{0:T(128)}, u32[]{:S(2)}) copy-start(f32[16]{0:T(128)} %copy-done.76) | copy-start | bytes 196
  244.6 18.1 %copy-start.67 = (f32[16]{0:T(128)S(1)}, f32[16]{0:T(128)}, u32[]{:S(2)}) copy-start(f32[16]{0:T(128)} %copy-done.66) | copy-start | bytes 196
  244.6 18.1 %copy-start.57 = (f32[16]{0:T(128)S(1)}, f32[16]{0:T(128)}, u32[]{:S(2)}) copy-start(f32[16]{0:T(128)} %copy-done.56) | copy-start | bytes 196
  244.6 18.1 %copy-start.68 = (f32[16,1]{0,1:T(1,128)S(1)}, f32[16,1]{0,1:T(1,128)}, u32[]{:S(2)}) copy-start(f32[16,1]{0,1:T(1,128)} %get-tuple-element.36) | copy-start | bytes 196
  244.6 18.1 %copy-start.69 = (f32[16,1]{0,1:T(1,128)S(1)}, f32[16,1]{0,1:T(1,128)}, u32[]{:S(2)}) copy-start(f32[16,1]{0,1:T(1,128)} %get-tuple-element.144) | copy-start | bytes 196
  244.6 18.1 %copy-start.70 = (f32[16,1]{0,1:T(1,128)S(1)}, f32[16,1]{0,1:T(1,128)}, u32[]{:S(2)}) copy-start(f32[16,1]{0,1:T(1,128)} %get-tuple-element.34) | copy-start | bytes 196
  244.6 18.1 %copy-start.73 = (f32[16,1]{0,1:T(1,128)S(1)}, f32[16,1]{0,1:T(1,128)}, u32[]{:S(2)}) copy-start(f32[16,1]{0,1:T(1,128)} %get-tuple-element.32) | copy-start | bytes 196
  244.6 18.1 %copy-start.74 = (f32[16,1]{0,1:T(1,128)S(1)}, f32[16,1]{0,1:T(1,128)}, u32[]{:S(2)}) copy-start(f32[16,1]{0,1:T(1,128)} %get-tuple-element.30) | copy-start | bytes 196
  244.6 18.1 %copy-start.75 = (f32[16,1]{0,1:T(1,128)S(1)}, f32[16,1]{0,1:T(1,128)}, u32[]{:S(2)}) copy-start(f32[16,1]{0,1:T(1,128)} %get-tuple-element.28) | copy-start | bytes 196
  244.7 18.0 %copy-start.55 = (f32[16]{0:T(128)S(1)}, f32[16]{0:T(128)}, u32[]{:S(2)}) copy-start(f32[16]{0:T(128)} %copy-done.54) | copy-start | bytes 196
  402.3 33.2 %all-to-all-start.4 = ((bf16[8,256,256]{1,2,0:T(8,128)(2,1)}), bf16[8,256,256]{1,2,0:T(8,128)(2,1)S(1)}, u32[]{:S(2)}, u32[]{:S(2)}) async-start(bf16[8,256,256]{1,2,0:T(8,128)(2,1)} %fusion.217), calls=%async_computation.4 | async-start | bytes 2097152 | tf_op jit(solution)/shard_map/all_to_all | solution.py:151
  435.7 24.4 %collective-permute-start.1 = (f32[256,256]{0,1:T(8,128)S(1)}, f32[256,256]{0,1:T(8,128)S(1)}, u32[]{:S(2)}, u32[]{:S(2)}) collective-permute-start(f32[256,256]{0,1:T(8,128)S(1)} %convert_reduce_fusion.1), channel_id=1, source_target_pairs={{0,0},{4,32},{8,64},{12,96},{16,128},{20,160},{24,192},{28,224},{3... | collective-permute-start | bytes 786440 | tf_op jit(solution)/shard_map/ppermute | solution.py:152
  (66 other events, 356.6 us)
Sparse Core Ops, SparseCore 0:
  28.5 33.5 all-gather.9
  96.3 117.3 all-gather.11
  254.2 46.5 all-gather.7
